TPU v7x, 32 devices: a whole 2x2x4 slice. The times are simulated.
32 devices in a mesh: ia: 4 (over z), ja: 4 (over y, x), ka: 2 (over core).
Axes of the slice: x: 2, y: 2, z: 4, core: 2. Of those that a mesh axis runs over, the one named last changes fastest.
Arguments:
- blocks: bfloat16 [4, 4, 4, 128, 128, 128], P('ia', 'ja', 'ka'), may hold values from -6 to 6
- coordinates: int32 [3, 4, 4, 4], P(None, 'ia', 'ja', 'ka'), may hold values from 0 to 3, as said below
- occupancy: int32 [4, 4, 4], P('ia', 'ja', 'ka'), may hold values from 0 to 1, as said below
- second_factor: bfloat16 [4, 512, 1024], P('ja', ('ia', 'ka')), may hold values from -12 to 12
- third_factor: bfloat16 [2, 512, 1024], P('ka', ('ia', 'ja')), may hold values from -0.0234375 to 0.0234375
- inverse_first: bfloat16 [1024, 1024], replicated
- inverse_second: bfloat16 [1024, 1024], replicated
Outputs:
- first_new: bfloat16 [4, 512, 1024], P('ia', ('ja', 'ka'))
- second_new: bfloat16 [4, 512, 1024], P('ja', ('ia', 'ka'))
Inputs may be any that keep to these rules, and one draw needn't show every extreme that they name: `occupancy`: each device has two slots; its second slot is occupied only where its first is. A device with two blocks is followed along ka, cyclically, by a device with none. Some device holds two blocks. coordinates[0], [1], [2] of a slot are a block row among 4, a block row among 4 and a block layer among 4 of its device's ranges; the two slots of a device name different layers.
All inputs are finite; a program needn't handle non-finite values.
Results may differ from a plain program's by a relative error of at most 0.006.
Values may be sent and summed in bfloat16 or wider, within the bound.
A program may use at most 128 MiB of HBM per device.

v0:
```python
import jax
import jax.numpy as jnp
from jax import lax
from jax.sharding import PartitionSpec as P

IB = 4
JB = 4


def passed_along(block, axis, distance):
    devices = range(lax.axis_size(axis))
    route = [((i - distance) % len(devices), i) for i in devices]
    return lax.ppermute(block, axis, route)


def block_products(tensor_block, left_rows, layer_slab, contract):
    block_edge = tensor_block.shape[0]
    step_rows = max(block_edge // 4, 1)
    summed = jnp.zeros((block_edge, left_rows.shape[1]), jnp.float32)
    for first_row in range(0, block_edge, step_rows):
        khatri = left_rows[first_row : first_row + step_rows][:, None, :] * layer_slab[None, :, :]
        if contract == 1:
            block_part = tensor_block[:, first_row : first_row + step_rows, :]
            contraction = (((1, 2), (0, 1)), ((), ()))
        else:
            block_part = tensor_block[first_row : first_row + step_rows]
            contraction = (((0, 2), (0, 1)), ((), ()))
        summed = summed + lax.dot_general(
            block_part, khatri, contraction, preferred_element_type=jnp.float32
        )
    return summed


def place_rows(partial_value, addend, block_index):
    block_edge = addend.shape[0]
    row_start = block_index * block_edge
    current = lax.dynamic_slice_in_dim(partial_value, row_start, block_edge, 0)
    return lax.dynamic_update_slice_in_dim(partial_value, addend, row_start, 0)


def pick_rows(source, block_index, block_edge):
    return lax.dynamic_slice_in_dim(source, block_index * block_edge, block_edge, 0)


def body(
    blocks, coordinates, occupancy, second_factor, third_factor, inverse_first, inverse_second
):
    block_edge = blocks.shape[-1]
    rank_width = inverse_first.shape[0]
    own_blocks = blocks.reshape(2, block_edge, block_edge, block_edge)
    places = coordinates.reshape(3, 2)
    occupied = occupancy.reshape(2)
    second_rows = lax.all_gather(second_factor, ("ia", "ka"), axis=1, tiled=True)[0]
    layer_rows = lax.all_gather(third_factor, ("ia", "ja"), axis=1, tiled=True)[0]
    slot_meta = jnp.stack([occupied[1], places[0, 1], places[1, 1]]).astype(jnp.bfloat16)
    arrived, arrived_layer, arrived_meta = passed_along(
        (own_blocks[1], pick_rows(layer_rows, places[2, 1], block_edge), slot_meta), "ka", 1
    )
    arrived_index = arrived_meta.astype(jnp.int32)
    keep_own = occupied[0] > 0
    tensor_block = jnp.where(keep_own, own_blocks[0], arrived)
    layer_slab = jnp.where(keep_own, pick_rows(layer_rows, places[2, 0], block_edge), arrived_layer)
    row_block = jnp.where(keep_own, places[0, 0], arrived_index[1])
    col_block = jnp.where(keep_own, places[1, 0], arrived_index[2])
    weight = jnp.where(keep_own, 1, arrived_index[0]).astype(jnp.float32)
    first_partial = jnp.zeros((IB * block_edge, rank_width), jnp.float32)
    contribution = block_products(
        tensor_block, pick_rows(second_rows, col_block, block_edge), layer_slab, 1
    )
    first_partial = place_rows(first_partial, contribution * weight, row_block)
    summed_rows = lax.psum(first_partial, ("ja", "ka"))
    first_rows = jnp.dot(
        summed_rows.astype(jnp.bfloat16), inverse_first, preferred_element_type=jnp.float32
    ).astype(jnp.bfloat16)
    share_rows = first_rows.shape[0] // lax.axis_size(("ja", "ka"))
    first_new = lax.dynamic_slice_in_dim(
        first_rows, lax.axis_index(("ja", "ka")) * share_rows, share_rows, 0
    )
    second_partial = jnp.zeros((JB * block_edge, rank_width), jnp.float32)
    contribution = block_products(
        tensor_block, pick_rows(first_rows, row_block, block_edge), layer_slab, 0
    )
    second_partial = place_rows(second_partial, contribution * weight, col_block)
    owned_second = lax.psum_scatter(
        second_partial[None], ("ia", "ka"), scatter_dimension=1, tiled=True
    )[0]
    second_new = jnp.dot(
        owned_second.astype(jnp.bfloat16), inverse_second, preferred_element_type=jnp.float32
    ).astype(jnp.bfloat16)
    return (first_new[None], second_new[None])


def solution(mesh):
    in_specs = (
        P("ia", "ja", "ka", None, None, None),
        P(None, "ia", "ja", "ka"),
        P("ia", "ja", "ka"),
        P("ja", ("ia", "ka"), None),
        P("ka", ("ia", "ja"), None),
        P(),
        P(),
    )
    out_specs = (P("ia", ("ja", "ka"), None), P("ja", ("ia", "ka"), None))
    return jax.shard_map(body, mesh=mesh, in_specs=in_specs, out_specs=out_specs, check_vma=False)
```

profile of v0, /device:TPU:0, one launch (start us, length us, event | category | flops | bytes accessed | tf_op | source)
XLA Modules:
  0.0 221.0 jit_solution(3574953310530504106)
XLA Ops:
  7.2 0.0 copy-start
  7.2 0.0 copy-start.5
  7.2 0.0 copy-start.4
  7.2 0.0 all-gather.5.cloned.1.call-start
  7.2 4.9 %slice_bitcast_fusion = bf16[128,128,128]{2,1,0:T(8,128)(2,1)} fusion(bf16[1,1,2,128,128,128]{5,4,3,2,1,0:T(8,128)(2,1)} %param.7), kind=kLoop, calls=%fused_computation.33 | loop fusion | bytes 8388608 | tf_op jit(solution)/shard_map/squeeze | solution.py:57
  12.1 0.5 collective-permute-start
  12.6 0.0 all-gather.5.cloned.1.call-update
  12.6 0.0 all-gather.3.cloned.1.call-start
  12.7 0.7 all-gather.3.cloned.1.call-update
  13.4 0.0 reduce-scatter.2.cloned.1.call-start
  13.4 0.0 copy-done.5
  13.5 0.6 slice.105
  14.1 0.0 copy-done.4
  14.1 0.6 fusion.98
  15.4 0.7 fusion.100
  16.0 54.2 %all-gather.5.cloned.1.call-done = bf16[1,512,1024]{2,1,0:T(8,128)(2,1)} async-done(((bf16[1,32,1024]{2,1,0:T(8,128)(2,1)}), bf16[1,512,1024]{2,1,0:T(8,128)(2,1)}) %all-gather.5.cloned.1.call-update) | async-done | bytes 1048592 | tf_op jit(solution)/shard_map/all_gather | solution.py:54
  70.3 1.0 dynamic-slice_bitcast_fusion
  71.2 0.1 collective-permute-start.2
  71.3 2.0 pad_maximum_fusion
  73.4 0.5 collective-permute-start.1
  74.5 0.1 collective-permute-done.1
  74.7 0.7 fusion.99
  78.5 14.5 %all-gather.3.cloned.1.call-done = bf16[1,512,1024]{2,1,0:T(8,128)(2,1)} async-done(((bf16[1,64,1024]{2,1,0:T(8,128)(2,1)}), bf16[1,512,1024]{2,1,0:T(8,128)(2,1)}) %all-gather.3.cloned.1.call-update) | async-done | bytes 1048592 | tf_op jit(solution)/shard_map/all_gather | solution.py:53
  93.0 1.0 dynamic-slice_bitcast_fusion.5
  93.9 0.0 collective-permute-done.2
  93.9 1.0 bitcast_select_fusion.1
  95.0 0.0 collective-permute-done
  95.0 2.6 %bitcast_select_fusion = bf16[128,128,128]{2,1,0:T(8,128)(2,1)S(1)} fusion(bf16[128,128,128]{2,1,0:T(8,128)(2,1)} %collective-permute-done, bf16[1,1,2,128,128,128]{5,4,3,2,1,0:T(8,128)(2,1)} %param.7, pred[]{:T(512)} %bitcast), kind=kLoop, calls=%fused_computation.16 | loop fusion | flops 2097152 | bytes 12582913 | tf_op jit(solution)/shard_map/jit(_where)/select_n | solution.py:61
  97.6 0.0 copy-start.1
  97.6 0.8 fusion.97
  98.4 1.3 fusion.47
  99.8 1.3 fusion.50
  101.1 1.3 fusion.53
  102.4 1.6 broadcast.9
  104.0 2.2 fusion.86
  106.2 58.6 %all-reduce.1 = bf16[512,1024]{1,0:T(8,128)(2,1)S(1)} all-reduce(f32[512,1024]{1,0:T(8,128)} %fusion.86), channel_id=1, replica_groups=mesh['ia'=4,'ja'=4,'ka'=2] {'ja','ka'}, use_global_device_ids=true, to_apply=%region_0.1 | all-reduce | flops 524288 | bytes 3145728 | tf_op jit(solution)/shard_map/psum | solution.py:71
  164.8 0.0 copy-done
  164.8 1.3 convolution_convert_fusion
  166.1 1.0 copy-done.3
  167.1 2.6 %fusion.35 = f32[128,1024]{1,0:T(8,128)S(1)} fusion(bf16[128,128,128]{2,1,0:T(8,128)(2,1)} %copy-done.1, bf16[32,1024]{1,0:T(8,128)(2,1)S(1)} %get-tuple-element.8, bf16[128,1024]{1,0:T(8,128)(2,1)S(1)} %bitcast_select_fusion.1), kind=kOutput, calls=%fused_computation.36 | convolution fusion | flops 1090519040 | bytes 5046272 | tf_op jit(solution)/shard_map/dot_general | solution.py:28
  169.7 1.3 fusion.38
  171.0 1.3 fusion.41
  172.4 1.6 broadcast_in_dim.9
  174.0 2.4 %fusion.77 = f32[1,512,1024]{2,1,0:T(8,128)} fusion(f32[1,512,1024]{2,1,0:T(8,128)} %broadcast_in_dim.9, s32[]{:T(128)S(6)} %select_n.47, f32[128,1024]{1,0:T(8,128)S(1)} %fusion.41, f32[128,1024]{1,0:T(8,128)S(1)} %fusion.38, f32[128,1024]{1,0:T(8,128)S(1)} %fusion.35, bf16[128,128,128]{2,1,0:T(8,128)(2,1)S(1)} %copy-done.2, ...), kind=kOutput, calls=%fused_computation.50 | convolution fusion | flops 1091043328 | bytes 6619144 | tf_op jit(solution)/shard_map/dot_general | solution.py:28
  176.3 0.0 reduce-scatter.2.cloned.1.call-update
  176.3 1.6 dynamic-slice_bitcast_fusion.1
  177.9 33.7 %reduce-scatter.2.cloned.1.call-done = f32[1,64,1024]{2,1,0:T(8,128)} async-done(((f32[1,512,1024]{2,1,0:T(8,128)}), f32[1,64,1024]{2,1,0:T(8,128)}) %reduce-scatter.2.cloned.1.call-update) | async-done | bytes 262160 | tf_op jit(solution)/shard_map/reduce_scatter | solution.py:84
  211.6 2.8 %fusion.89 = bf16[1,64,1024]{2,1,0:T(8,128)(2,1)} fusion(bf16[1024,1024]{1,0:T(8,128)(2,1)} %param.13, f32[1,64,1024]{2,1,0:T(8,128)} %reduce-scatter.2.cloned.1.call-done), kind=kOutput, calls=%fused_computation.55 | convolution fusion | flops 134348800 | bytes 2490368 | tf_op jit(solution)/shard_map/dot_general | solution.py:87
  (8 shorter events, 0.0 us)
Async XLA Ops:
  7.2 157.6 %copy-start = (bf16[1024,1024]{1,0:T(8,128)(2,1)S(1)}, bf16[1024,1024]{1,0:T(8,128)(2,1)}, u32[]{:S(2)}) copy-start(bf16[1024,1024]{1,0:T(8,128)(2,1)} %param.12) | copy-start | bytes 6291460
  7.2 6.3 %copy-start.5 = (s32[1,1,2]{2,1,0:T(1,128)S(1)}, s32[1,1,2]{2,1,0:T(1,128)}, u32[]{:S(2)}) copy-start(s32[1,1,2]{2,1,0:T(1,128)} %param.9) | copy-start | bytes 28
  7.2 6.9 %copy-start.4 = (s32[3,1,1,2]{0,3,2,1:T(2,128)S(1)}, s32[3,1,1,2]{0,3,2,1:T(2,128)}, u32[]{:S(2)}) copy-start(s32[3,1,1,2]{0,3,2,1:T(2,128)} %param.8) | copy-start | bytes 76
  7.2 63.1 %all-gather.5.cloned.1.call-start = ((), (), s32[]{:S(2)}) async-start(), calls=%async_computation.2 | async-start | bytes 1114112 | tf_op jit(solution)/shard_map/all_gather | solution.py:54
  12.1 82.9 %collective-permute-start = (bf16[128,128,128]{2,1,0:T(8,128)(2,1)}, bf16[128,128,128]{2,1,0:T(8,128)(2,1)}, u32[]{:S(2)}, u32[]{:S(2)}) collective-permute-start(bf16[128,128,128]{2,1,0:T(8,128)(2,1)} %slice_bitcast_fusion), channel_id=1, source_target_pairs={{1,0},{0,1},{3,2},{2,3},{5,4},{4,5},{7,6},{6,7},{9,8},{8,9},{11,10... | collective-permute-start | bytes 12582920 | tf_op jit(solution)/shard_map/ppermute | solution.py:13
  12.6 80.3 %all-gather.3.cloned.1.call-start = ((), (), s32[]{:S(2)}) async-start(), calls=%async_computation.1 | async-start | bytes 1179648 | tf_op jit(solution)/shard_map/all_gather | solution.py:53
  13.4 198.2 %reduce-scatter.2.cloned.1.call-start = ((), (), s32[]{:S(2)}) async-start(), calls=%async_computation.3 | async-start | bytes 2359296 | tf_op jit(solution)/shard_map/reduce_scatter | solution.py:84
  71.2 22.7 %collective-permute-start.2 = (bf16[128,1024]{1,0:T(8,128)(2,1)S(1)}, bf16[128,1024]{1,0:T(8,128)(2,1)S(1)}, u32[]{:S(2)}, u32[]{:S(2)}) collective-permute-start(bf16[128,1024]{1,0:T(8,128)(2,1)S(1)} %dynamic-slice_bitcast_fusion), channel_id=1, source_target_pairs={{1,0},{0,1},{3,2},{2,3},{5,4},{4,5},{7,6},{6,7},{9,8},{8,9},{11,10... | collective-permute-start | bytes 786440 | tf_op jit(solution)/shard_map/ppermute | solution.py:13
  73.4 1.3 collective-permute-start.1
  97.6 2.2 copy-start.1
  166.1 1.0 copy-start.3
  167.0 2.7 %copy-start.2 = (bf16[128,128,128]{2,1,0:T(8,128)(2,1)S(1)}, bf16[128,128,128]{2,1,0:T(8,128)(2,1)}, u32[]{:S(2)}) copy-start(bf16[128,128,128]{2,1,0:T(8,128)(2,1)} %copy-done.1) | copy-start | bytes 12582916
Sparse Core Ops, SparseCore 0:
  12.8 57.4 all-gather.4
  71.9 21.0 all-gather.2
  176.5 35.1 reduce-scatter.1
where the time goes:
time: 221 us
  waiting for transfers between devices  103 us (47%)
  blocking collectives  58.6 us (27%)
  between operations  18.5 us (8%)
  matrix products  17.8 us (8%)
  local copies, waits for them, and re-layouts  16 us (7%)
  other arithmetic  5.71 us (3%)
    psum x1, blocking collectives, body(): summed_rows = lax.psum(first_partial, ('ja', 'ka'))  58.6 us
    all_gather x1, waiting for transfers between devices, body(): lax.all_gather(third_factor, ('ia', 'ja'), axis=1, tiled=True)[0]  54.2 us
    reduce_scatter x1, waiting for transfers between devices, body(): lax.psum_scatter(second_partial[None], ('ia', 'ka'), scatter_dimension=1,...  33.7 us
    all_gather x1, waiting for transfers between devices, body(): lax.all_gather(second_factor, ('ia', 'ka'), axis=1, tiled=True)[0]  14.5 us
    dot_general x8, matrix products, block_products(): lax.dot_general(block_part, khatri, contraction, preferred_element_type=j...  13.7 us
    squeeze x1, local copies, waits for them, and re-layouts, body(): own_blocks[1]  4.87 us
  transfers between devices with their start and end apart: 6, of which 4 were waited for; matrix products, arithmetic and copies ran while one was open for 4% of the time, Pallas kernels for 0%

commit v1 on v0

v1 whole, which is shorter than its diff:
```python
import functools

import jax
import jax.numpy as jnp
from jax import lax
from jax.experimental import pallas as pl
from jax.experimental.pallas import tpu as pltpu
from jax.sharding import PartitionSpec as P

IB = 4
JB = 4
TILES = 4
MESH = pl.DeviceIdType.MESH
AXES = ("ia", "ja", "ka")


def kernel(
    sizes,
    blocks,
    places,
    occupied,
    second_in,
    third_in,
    inverse_first,
    inverse_second,
    first_out,
    second_out,
    xbuf,
    inv1,
    inv2,
    meta_s,
    meta_r,
    cbuf,
    bbuf,
    slab_s,
    slab_r,
    cuse,
    buse,
    tbuf,
    oacc,
    d1s,
    d1r,
    keep1,
    p1s,
    p1r,
    own1,
    fr1,
    abuf,
    d2s,
    d2r,
    keep2,
    p2s,
    p2r,
    own2,
    fr2,
    local_sem,
    once_send,
    once_recv,
    z_send,
    z_recv,
    y_send,
    y_recv,
    k_send,
    k_recv,
):
    na, nb, nc = sizes
    tiles, edge, width = slab_s.shape
    rs, rt = bbuf.shape[3], cbuf.shape[3]
    sh1, sh2 = abuf.shape[3], own2.shape[1]
    a, b, c = (lax.axis_index(name) for name in AXES)
    sent = []

    def away(axis, d):
        n = sizes[AXES.index(axis)]
        me = (a, b, c)[AXES.index(axis)]
        return lax.rem(me + d, n)

    def send(src, dst, send_sem, recv_sem, axis, d):
        copy = pltpu.make_async_remote_copy(
            src_ref=src,
            dst_ref=dst,
            send_sem=send_sem,
            recv_sem=recv_sem,
            device_id={axis: away(axis, d)},
            device_id_type=MESH,
        )
        copy.start()
        sent.append(copy)
        return copy

    def cols(t):
        return pl.ds(t * width, width)

    local = []

    def local_copy(src, dst):
        copy = pltpu.make_async_copy(src, dst, local_sem.at[len(local)])
        copy.start()
        local.append(copy)
        return copy

    own_third = [
        local_copy(third_in.at[0, :, cols(t)], cbuf.at[t, a, b]) for t in range(tiles)
    ]
    own_second = [
        local_copy(second_in.at[0, :, cols(t)], bbuf.at[t, a, c]) for t in range(tiles)
    ]
    own_block = local_copy(blocks.at[0, 0, 0], xbuf.at[0])
    got_inv1 = local_copy(inverse_first, inv1)
    got_inv2 = local_copy(inverse_second, inv2)

    barrier = pltpu.get_barrier_semaphore()
    for axis, n in zip(AXES, sizes):
        for d in range(1, n):
            pl.semaphore_signal(
                barrier, inc=1, device_id={axis: away(axis, d)}, device_id_type=MESH
            )
    keep = occupied[0, 0, 0] > 0
    row0, col0, layer0 = (places[m, 0, 0, 0] for m in range(3))
    row1, col1, layer1 = (places[m, 0, 0, 1] for m in range(3))
    weight1 = jnp.where(occupied[0, 0, 1] > 0, 1.0, 0.0).astype(jnp.float32)
    for q in range(IB):
        value = jnp.where(row1 == q, weight1, 0.0)
        meta_s[pl.ds(q, 1), :] = jnp.full((1, width), value, jnp.float32)
    for q in range(JB):
        value = jnp.where(col1 == q, weight1, 0.0)
        meta_s[pl.ds(IB + q, 1), :] = jnp.full((1, width), value, jnp.float32)
    pl.semaphore_wait(barrier, (na - 1) + (nb - 1) + (nc - 1))

    def chosen(own_value, row):
        own = jnp.where(own_value, 1.0, 0.0).astype(jnp.float32)
        return jnp.where(keep, jnp.full((1, width), own, jnp.float32), meta_r[pl.ds(row, 1), :]) > 0.5

    def third_column(t):
        return [
            send(
                third_in.at[0, :, cols(t)],
                cbuf.at[t, a, b],
                z_send.at[0, t, d - 1],
                z_recv.at[0, t, d - 1],
                "ia",
                d,
            )
            for d in range(1, na)
        ]

    def second_column(t):
        return [
            send(
                second_in.at[0, :, cols(t)],
                bbuf.at[t, a, c],
                z_send.at[1, t, d - 1],
                z_recv.at[1, t, d - 1],
                "ia",
                d,
            )
            for d in range(1, na)
        ]

    third_z, second_z = {}, {}
    third_z[0] = third_column(0)
    block_copy = send(blocks.at[0, 0, 1], xbuf.at[1], once_send.at[0], once_recv.at[0], "ka", 1)
    meta_copy = send(meta_s, meta_r, once_send.at[1], once_recv.at[1], "ka", 1)
    for t in range(1, tiles):
        third_z[t] = third_column(t)
        second_z[t - 1] = second_column(t - 1)
    second_z[tiles - 1] = second_column(tiles - 1)

    third_y, second_k, slab_copy = {}, {}, {}

    def spread_third(t):
        own_third[t].wait()
        for copy in third_z[t]:
            copy.wait_recv()
        third_y[t] = [
            send(
                cbuf.at[t, :, b],
                cbuf.at[t, :, b],
                y_send.at[0, t, d - 1],
                y_recv.at[0, t, d - 1],
                "ja",
                d,
            )
            for d in range(1, nb)
        ]

    def spread_second(t):
        own_second[t].wait()
        for copy in second_z[t]:
            copy.wait_recv()
        second_k[t] = [
            send(
                bbuf.at[t, :, c],
                bbuf.at[t, :, c],
                k_send.at[0, t, d - 1],
                k_recv.at[0, t, d - 1],
                "ka",
                d,
            )
            for d in range(1, nc)
        ]

    def layer_piece(t, layer, piece):
        per = edge // rt
        total = na * nb * rt // edge
        value = None
        for q in range(total):
            s = q * per + piece
            rows = cbuf[t, s // nb, s % nb]
            value = rows if value is None else jnp.where(layer == q, rows, value)
        return value

    def pass_slab(t):
        for copy in third_y[t]:
            copy.wait_recv()
        for piece in range(edge // rt):
            slab_s[t, pl.ds(piece * rt, rt), :] = layer_piece(t, layer1, piece)
        slab_copy[t] = send(
            slab_s.at[t], slab_r.at[t], k_send.at[1, t, 0], k_recv.at[1, t, 0], "ka", 1
        )
        for piece in range(edge // rt):
            cuse[pl.ds(piece * rt, rt), :] = layer_piece(t, layer0, piece)

    def first_products(t):
        for copy in second_k[t]:
            copy.wait_recv()
        if t == 0:
            own_block.wait()
            block_copy.wait_recv()
            meta_copy.wait_recv()
        masks = [chosen(col0 == q, IB + q) for q in range(JB)]
        per = edge // rs
        for piece in range(per):
            value = jnp.zeros((rs, width), jnp.float32)
            for q in range(JB):
                s = q * per + piece
                rows = bbuf[t, s // nc, s % nc].astype(jnp.float32)
                value = jnp.where(masks[q], rows, value)
            buse[pl.ds(piece * rs, rs), :] = value
        slab_copy[t].wait_recv()
        cuse[...] = jnp.where(keep, cuse[...], slab_r[t])
        slot = jnp.where(keep, 0, 1)

        def eight(step, carry):
            base = pl.multiple_of(step * 8, 8)
            sums = []
            for u in range(8):
                product = jnp.dot(
                    xbuf[slot, base + u], cuse[...], preferred_element_type=jnp.float32
                )
                tbuf[t, base + u] = product.astype(jnp.bfloat16)
                sums.append(jnp.sum(product * buse[...], axis=0, keepdims=True))
            oacc[pl.ds(base, 8), :] = jnp.concatenate(sums, axis=0)
            return carry

        lax.fori_loop(0, edge // 8, eight, 0)

    def owned_piece(owner, rows, own_place, meta_row):
        start = owner * rows
        block = start // edge
        off = pl.multiple_of(start % edge, rows)
        mask = chosen(own_place == block, meta_row + block)
        return jnp.where(mask, oacc[pl.ds(off, rows), :], 0.0)

    def pair_sums(t, n, rows, own_place, meta_row, outgoing, arriving, kept, kind):
        copies = []
        for d in range(1, nc):
            for m in range(n):
                owner = m * nc + away("ka", d)
                outgoing[t, d - 1, m] = owned_piece(owner, rows, own_place, meta_row).astype(
                    jnp.bfloat16
                )
            copies.append(
                send(
                    outgoing.at[t, d - 1],
                    arriving.at[t, d - 1],
                    k_send.at[kind, t, d - 1],
                    k_recv.at[kind, t, d - 1],
                    "ka",
                    d,
                )
            )
        for m in range(n):
            kept[t, m] = owned_piece(m * nc + c, rows, own_place, meta_row)
        return copies

    def chip_sums(t, axis, n, copies, arriving, kept, outgoing, landing, own, sends, recvs, kind):
        for copy in copies:
            copy.wait_recv()
        started = []
        for d in range(n):
            m = away(axis, d)
            value = kept[t, m]
            for e in range(1, nc):
                value = value + arriving[t, e - 1, m].astype(jnp.float32)
            if d == 0:
                own[t] = value
            else:
                outgoing[t, d - 1] = value.astype(jnp.bfloat16)
                started.append(
                    send(
                        outgoing.at[t, d - 1],
                        landing.at[t, d - 1],
                        sends.at[kind, t, d - 1],
                        recvs.at[kind, t, d - 1],
                        axis,
                        d,
                    )
                )
        return started

    first_k, first_y = {}, {}

    def first_chip_sums(t):
        first_y[t] = chip_sums(
            t, "ja", nb, first_k[t], d1r, keep1, p1s, p1r, own1, y_send, y_recv, 1
        )

    spread_third(0)
    spread_second(0)
    for t in range(tiles):
        if t + 1 < tiles:
            spread_third(t + 1)
        pass_slab(t)
        if t:
            first_chip_sums(t - 1)
        first_products(t)
        first_k[t] = pair_sums(t, nb, sh1, row0, 0, d1s, d1r, keep1, 2)
        if t + 1 < tiles:
            spread_second(t + 1)
    first_chip_sums(tiles - 1)

    def gathered(t, copies, own, landing, n):
        for copy in copies:
            copy.wait_recv()
        value = own[t]
        for d in range(1, n):
            value = value + landing[t, d - 1].astype(jnp.float32)
        return value.astype(jnp.bfloat16)

    for t in range(tiles):
        fr1[:, cols(t)] = gathered(t, first_y[t], own1, p1r, nb)
    got_inv1.wait()
    new_y, new_k = {}, {}
    for t in range(tiles):
        value = jnp.dot(fr1[...], inv1[:, cols(t)], preferred_element_type=jnp.float32)
        value = value.astype(jnp.bfloat16)
        abuf[t, b, c] = value
        first_out[0, :, cols(t)] = value
        new_y[t] = [
            send(
                abuf.at[t, b, c],
                abuf.at[t, b, c],
                y_send.at[2, t, d - 1],
                y_recv.at[2, t, d - 1],
                "ja",
                d,
            )
            for d in range(1, nb)
        ]

    def spread_new(t):
        for copy in new_y[t]:
            copy.wait_recv()
        new_k[t] = [
            send(
                abuf.at[t, :, c],
                abuf.at[t, :, c],
                k_send.at[3, t, d - 1],
                k_recv.at[3, t, d - 1],
                "ka",
                d,
            )
            for d in range(1, nc)
        ]

    def second_products(t):
        for copy in new_k[t]:
            copy.wait_recv()
        masks = [chosen(row0 == q, q) for q in range(IB)]
        per = edge // sh1
        for piece in range(per):
            value = jnp.zeros((sh1, width), jnp.float32)
            for q in range(IB):
                s = q * per + piece
                rows = abuf[t, s // nc, s % nc].astype(jnp.float32)
                value = jnp.where(masks[q], rows, value)
            buse[pl.ds(piece * sh1, sh1), :] = value
        lanes = 128
        for lane in range(0, width, lanes):

            def eight(step, total):
                base = pl.multiple_of(step * 8, 8)
                rows = buse[pl.ds(base, 8), pl.ds(lane, lanes)]
                for u in range(8):
                    total = total + rows[u : u + 1] * tbuf[t, base + u, :, pl.ds(lane, lanes)].astype(
                        jnp.float32
                    )
                return total

            oacc[:, pl.ds(lane, lanes)] = lax.fori_loop(
                0, edge // 8, eight, jnp.zeros((edge, lanes), jnp.float32)
            )

    second_s, second_y = {}, {}

    def second_chip_sums(t):
        second_y[t] = chip_sums(
            t, "ia", na, second_s[t], d2r, keep2, p2s, p2r, own2, z_send, z_recv, 2
        )

    spread_new(0)
    for t in range(tiles):
        if t + 1 < tiles:
            spread_new(t + 1)
        second_products(t)
        second_s[t] = pair_sums(t, na, sh2, col0, IB, d2s, d2r, keep2, 4)
        if t:
            second_chip_sums(t - 1)
    second_chip_sums(tiles - 1)
    for t in range(tiles):
        fr2[:, cols(t)] = gathered(t, second_y[t], own2, p2r, na)
    got_inv2.wait()
    for t in range(tiles):
        value = jnp.dot(fr2[...], inv2[:, cols(t)], preferred_element_type=jnp.float32)
        second_out[0, :, cols(t)] = value.astype(jnp.bfloat16)
    for copy in sent:
        copy.wait_send()


def body(
    sizes,
    blocks,
    coordinates,
    occupancy,
    second_factor,
    third_factor,
    inverse_first,
    inverse_second,
):
    na, nb, nc = sizes
    edge, rank = blocks.shape[-1], inverse_first.shape[0]
    tiles = TILES
    width = rank // tiles
    rs, rt = second_factor.shape[1], third_factor.shape[1]
    sh1, sh2 = IB * edge // (nb * nc), JB * edge // (na * nc)
    bf16, f32 = jnp.bfloat16, jnp.float32
    dma = pltpu.SemaphoreType.DMA
    widest_k = max(nc - 1, 1)
    vmem = pl.BlockSpec(memory_space=pltpu.VMEM)
    smem = pl.BlockSpec(memory_space=pltpu.SMEM)
    anywhere = pl.BlockSpec(memory_space=pl.ANY)
    scratch = [
        pltpu.VMEM((2, edge, edge, edge), bf16),
        pltpu.VMEM((rank, rank), bf16),
        pltpu.VMEM((rank, rank), bf16),
        pltpu.VMEM((IB + JB, width), f32),
        pltpu.VMEM((IB + JB, width), f32),
        pltpu.VMEM((tiles, na, nb, rt, width), bf16),
        pltpu.VMEM((tiles, na, nc, rs, width), bf16),
        pltpu.VMEM((tiles, edge, width), bf16),
        pltpu.VMEM((tiles, edge, width), bf16),
        pltpu.VMEM((edge, width), bf16),
        pltpu.VMEM((edge, width), f32),
        pltpu.VMEM((tiles, edge, edge, width), bf16),
        pltpu.VMEM((edge, width), f32),
        pltpu.VMEM((tiles, nc - 1, nb, sh1, width), bf16),
        pltpu.VMEM((tiles, nc - 1, nb, sh1, width), bf16),
        pltpu.VMEM((tiles, nb, sh1, width), f32),
        pltpu.VMEM((tiles, nb - 1, sh1, width), bf16),
        pltpu.VMEM((tiles, nb - 1, sh1, width), bf16),
        pltpu.VMEM((tiles, sh1, width), f32),
        pltpu.VMEM((sh1, rank), bf16),
        pltpu.VMEM((tiles, nb, nc, sh1, width), bf16),
        pltpu.VMEM((tiles, nc - 1, na, sh2, width), bf16),
        pltpu.VMEM((tiles, nc - 1, na, sh2, width), bf16),
        pltpu.VMEM((tiles, na, sh2, width), f32),
        pltpu.VMEM((tiles, na - 1, sh2, width), bf16),
        pltpu.VMEM((tiles, na - 1, sh2, width), bf16),
        pltpu.VMEM((tiles, sh2, width), f32),
        pltpu.VMEM((sh2, rank), bf16),
        dma((2 * tiles + 3,)),
        dma((2,)),
        dma((2,)),
        dma((3, tiles, na - 1)),
        dma((3, tiles, na - 1)),
        dma((3, tiles, nb - 1)),
        dma((3, tiles, nb - 1)),
        dma((5, tiles, widest_k)),
        dma((5, tiles, widest_k)),
    ]
    return pl.pallas_call(
        functools.partial(kernel, sizes),
        name="als",
        out_shape=(
            jax.ShapeDtypeStruct((1, sh1, rank), bf16),
            jax.ShapeDtypeStruct((1, sh2, rank), bf16),
        ),
        in_specs=[anywhere, smem, smem, vmem, vmem, anywhere, anywhere],
        out_specs=(vmem, vmem),
        scratch_shapes=scratch,
        compiler_params=pltpu.CompilerParams(
            collective_id=0, has_side_effects=True, vmem_limit_bytes=67043328
        ),
    )(blocks, coordinates, occupancy, second_factor, third_factor, inverse_first, inverse_second)


def solution(mesh):
    sizes = tuple(mesh.shape[name] for name in AXES)
    in_specs = (
        P("ia", "ja", "ka", None, None, None),
        P(None, "ia", "ja", "ka"),
        P("ia", "ja", "ka"),
        P("ja", ("ia", "ka"), None),
        P("ka", ("ia", "ja"), None),
        P(),
        P(),
    )
    out_specs = (P("ia", ("ja", "ka"), None), P("ja", ("ia", "ka"), None))
    return jax.shard_map(
        functools.partial(body, sizes),
        mesh=mesh,
        in_specs=in_specs,
        out_specs=out_specs,
        check_vma=False,
    )
```

time: 221 us -> 75.7 us (0.34)
  waiting for transfers between devices: 103 us -> 0 us
  Pallas kernels: 0 us -> 70.4 us
  blocking collectives: 58.6 us -> 0 us
  between operations: 18.5 us -> 0.64 us
  matrix products: 17.8 us -> 0 us
  local copies, waits for them, and re-layouts: 16 us -> 4.46 us
  other arithmetic: 5.71 us -> 0 us
    pallas_call x0 -> x1, Pallas kernels: none -> 70.4 us  [body(): pl.pallas_call(functools.partial(kernel, sizes), name='als', out_shape=(j...]
    all_gather x2 -> x0, waiting for transfers between devices: 68.7 us -> none  [the longest x1 54.2 us: body(): lax.all_gather(third_factor, ('ia', 'ja'), axis=1, tiled=True)[0]]
    psum x1 -> x0, blocking collectives: 58.6 us -> none  [body(): summed_rows = lax.psum(first_partial, ('ja', 'ka'))]
    reduce_scatter x1 -> x0, waiting for transfers between devices: 33.7 us -> none  [body(): lax.psum_scatter(second_partial[None], ('ia', 'ka'), scatter_dimension=1,...]
    dot_general x10 -> x0, matrix products: 17.8 us -> none  [the longest x8 13.7 us: block_products(): lax.dot_general(block_part, khatri, contraction, preferred_element_type=j...]
    squeeze x1 -> x0, local copies, waits for them, and re-layouts: 4.87 us -> none  [body(): own_blocks[1]]
    select_n x2 -> x0, other arithmetic: 3.66 us -> none  [the longest x1 2.63 us: body(): tensor_block = jnp.where(keep_own, own_blocks[0], arrived)]
    unnamed x12 -> x3, local copies, waits for them, and re-layouts: 0.99 us -> 4.46 us
  transfers between devices with their start and end apart: 6 -> 0, of which waited for: 4 -> 0; matrix products, arithmetic and copies ran while one was open for 4% -> 0% of each run, Pallas kernels for 0% -> 0%
where the time goes in v1:
time: 75.7 us; the launch traced here: 75.5 us
  Pallas kernels  70.4 us (93%)
  local copies, waits for them, and re-layouts  4.46 us (6%)
    pallas_call x1, Pallas kernels, body(): pl.pallas_call(functools.partial(kernel, sizes), name='als', out_shape=(j...  70.4 us
    unnamed x3, local copies, waits for them, and re-layouts  4.46 us

profile of v1, /device:TPU:0, one launch (start us, length us, event | category | flops | bytes accessed | tf_op | source)
XLA Modules:
  0.0 75.5 jit_solution(11831533854702406486)
XLA Ops:
  0.6 1.3 %copy.9.places = s32[3,1,1,2]{3,2,1,0:T(1,128)} copy(s32[3,1,1,2]{0,3,2,1:T(2,128)} %param.8) | data formatting | bytes 48 | tf_op args[1]
  2.0 70.4 %als.1 = (bf16[1,64,1024]{2,1,0:T(8,128)(2,1)}, bf16[1,64,1024]{2,1,0:T(8,128)(2,1)}) custom-call(bf16[1,1,2,128,128,128]{5,4,3,2,1,0:T(8,128)(2,1)} %blocks.1, s32[3,1,1,2]{3,2,1,0:T(1,128)} %copy.9.places, s32[1,1,2]{2,1,0:T(1,128)} %occupied.1, bf16[1,64,1024]{2,1,0:T(8,128)(2,1)} %second_in.1, bf16[1,32,1024]{2,1,0:T(8,128)(2,1)} %third_in.1, ...), custom_call_target="tpu_custom_call" | custom-call | tf_op jit(solution)/shard_map/als/pallas_call | solution.py:492
  72.4 1.6 %copy.12 = bf16[1,64,1024]{2,1,0:T(8,128)(2,1)} copy(bf16[1,64,1024]{2,1,0:T(8,128)(2,1)} %get-tuple-element.4) | data formatting | bytes 262144
  74.0 1.6 %copy.13 = bf16[1,64,1024]{2,1,0:T(8,128)(2,1)} copy(bf16[1,64,1024]{2,1,0:T(8,128)(2,1)} %get-tuple-element.5) | data formatting | bytes 262144

commit v2 on v1

--- a/solution.py
+++ b/solution.py
@@ -17,8 +17,8 @@
 def kernel(
     sizes,
     blocks,
-    places,
-    occupied,
+    places_in,
+    occupied_in,
     second_in,
     third_in,
     inverse_first,
@@ -53,6 +53,8 @@
     p2r,
     own2,
     fr2,
+    places,
+    occupied,
     local_sem,
     once_send,
     once_recv,
@@ -99,6 +101,8 @@
         local.append(copy)
         return copy
 
+    got_places = local_copy(places_in, places)
+    got_occupied = local_copy(occupied_in, occupied)
     own_third = [
         local_copy(third_in.at[0, :, cols(t)], cbuf.at[t, a, b]) for t in range(tiles)
     ]
@@ -115,6 +119,8 @@
             pl.semaphore_signal(
                 barrier, inc=1, device_id={axis: away(axis, d)}, device_id_type=MESH
             )
+    got_places.wait()
+    got_occupied.wait()
     keep = occupied[0, 0, 0] > 0
     row0, col0, layer0 = (places[m, 0, 0, 0] for m in range(3))
     row1, col1, layer1 = (places[m, 0, 0, 1] for m in range(3))
@@ -448,7 +454,6 @@
     dma = pltpu.SemaphoreType.DMA
     widest_k = max(nc - 1, 1)
     vmem = pl.BlockSpec(memory_space=pltpu.VMEM)
-    smem = pl.BlockSpec(memory_space=pltpu.SMEM)
     anywhere = pl.BlockSpec(memory_space=pl.ANY)
     scratch = [
         pltpu.VMEM((2, edge, edge, edge), bf16),
@@ -479,7 +484,9 @@
         pltpu.VMEM((tiles, na - 1, sh2, width), bf16),
         pltpu.VMEM((tiles, sh2, width), f32),
         pltpu.VMEM((sh2, rank), bf16),
-        dma((2 * tiles + 3,)),
+        pltpu.SMEM(coordinates.shape, jnp.int32),
+        pltpu.SMEM(occupancy.shape, jnp.int32),
+        dma((2 * tiles + 5,)),
         dma((2,)),
         dma((2,)),
         dma((3, tiles, na - 1)),
@@ -489,20 +496,32 @@
         dma((5, tiles, widest_k)),
         dma((5, tiles, widest_k)),
     ]
-    return pl.pallas_call(
+    results = pl.pallas_call(
         functools.partial(kernel, sizes),
         name="als",
         out_shape=(
             jax.ShapeDtypeStruct((1, sh1, rank), bf16),
             jax.ShapeDtypeStruct((1, sh2, rank), bf16),
         ),
-        in_specs=[anywhere, smem, smem, vmem, vmem, anywhere, anywhere],
+        in_specs=[anywhere, anywhere, anywhere, vmem, vmem, anywhere, anywhere],
         out_specs=(vmem, vmem),
         scratch_shapes=scratch,
         compiler_params=pltpu.CompilerParams(
             collective_id=0, has_side_effects=True, vmem_limit_bytes=67043328
         ),
     )(blocks, coordinates, occupancy, second_factor, third_factor, inverse_first, inverse_second)
+    return pl.pallas_call(
+        hand_over,
+        name="hand_over",
+        out_shape=tuple(jax.ShapeDtypeStruct(x.shape, x.dtype) for x in results),
+        in_specs=[vmem, vmem],
+        out_specs=(vmem, vmem),
+    )(*results)
+
+
+def hand_over(first_in, second_in, first_out, second_out):
+    first_out[...] = first_in[...]
+    second_out[...] = second_in[...]
 
 
 def solution(mesh):

time: 75.7 us -> 74.2 us (0.980)
  local copies, waits for them, and re-layouts: 4.46 us -> 1.32 us
  Pallas kernels: 70.4 us -> 72.1 us
    unnamed x3 -> x1, local copies, waits for them, and re-layouts: 4.46 us -> 1.32 us
    pallas_call x0 -> x1, Pallas kernels: none -> 1.68 us  [body(): pl.pallas_call(hand_over, name='hand_over', out_shape=tuple((jax.ShapeDty...]
where the time goes in v2:
time: 74.2 us; the launch traced here: 74 us
  Pallas kernels  72.1 us (97%)
  local copies, waits for them, and re-layouts  1.32 us (2%)
    pallas_call x1, Pallas kernels, body(): pl.pallas_call(functools.partial(kernel, sizes), name='als', out_shape=(j...  70.4 us
    pallas_call x1, Pallas kernels, body(): pl.pallas_call(hand_over, name='hand_over', out_shape=tuple((jax.ShapeDty...  1.68 us

profile of v2, /device:TPU:0, one launch (start us, length us, event | category | flops | bytes accessed | tf_op | source)
XLA Modules:
  0.0 74.0 jit_solution(5141574636573736816)
XLA Ops:
  0.6 1.3 %copy.9.places_in = s32[3,1,1,2]{3,2,1,0:T(1,128)} copy(s32[3,1,1,2]{0,3,2,1:T(2,128)} %param.8) | data formatting | bytes 48 | tf_op args[1]
  1.9 70.4 %als.1 = (bf16[1,64,1024]{2,1,0:T(8,128)(2,1)}, bf16[1,64,1024]{2,1,0:T(8,128)(2,1)}) custom-call(bf16[1,1,2,128,128,128]{5,4,3,2,1,0:T(8,128)(2,1)} %blocks.1, s32[3,1,1,2]{3,2,1,0:T(1,128)} %copy.9.places_in, s32[1,1,2]{2,1,0:T(1,128)} %occupied_in.1, bf16[1,64,1024]{2,1,0:T(8,128)(2,1)} %second_in.1, bf16[1,32,1024]{2,1,0:T(8,128)(2,1)} %third_in.1, ...), custom_call_target="tpu_custom_call" | custom-call | tf_op jit(solution)/shard_map/als/pallas_call | solution.py:499
  72.4 1.7 %hand_over.1 = (bf16[1,64,1024]{2,1,0:T(8,128)(2,1)}, bf16[1,64,1024]{2,1,0:T(8,128)(2,1)}) custom-call(bf16[1,64,1024]{2,1,0:T(8,128)(2,1)} %get-tuple-element.4.first_in, bf16[1,64,1024]{2,1,0:T(8,128)(2,1)} %get-tuple-element.5.second_in), custom_call_target="tpu_custom_call" | custom-call | tf_op jit(solution)/shard_map/hand_over/pallas_call | solution.py:513
